TPU v7x, 512 devices: a whole 4x4x16 slice. The times are simulated.
512 devices in a mesh: seq: 16 (over x, y_hi, core), head: 32 (over z, y_lo).
Axes of the slice: x: 4, y: 4 (y_hi: 2, y_lo: 2; y = y_hi * 2 + y_lo), z: 16, core: 2. Of those that a mesh axis runs over, the one named last changes fastest.
Arguments:
- x_inner: bfloat16 [24576, 16384], P('seq', 'head'), may hold values from -400 to 400
- z_gate: bfloat16 [24576, 16384], P('seq', 'head'), may hold values from -6 to 6
- bc_raw: bfloat16 [24576, 512], P(('seq', 'head')), may hold values from -6 to 6
- conv_weight: float32 [4, 512], replicated, may hold values from -3 to 3
- conv_bias: float32 [512], replicated, may hold values from -3 to 3
- dt_raw: float32 [24576, 128], P('seq', 'head'), may hold values from -6 to 24576
- a_log: float32 [128], P('head'), may hold values from -20 to 1
- d_skip: float32 [128], P('head'), may hold values from 0.5 to 1.5
- norm_gain: float32 [16384], P('head'), may hold values from 0.5 to 1.5
Outputs:
- mixer_out: bfloat16 [24576, 16384], P('seq', 'head')
All inputs are finite; a program needn't handle non-finite values.
Results may differ from a plain program's by a relative error of at most 0.0034.
Values may be sent and summed in bfloat16 or wider, within the bound.
A program may use at most 64 MiB of HBM per device.

v0:
```python
import jax
import jax.numpy as jnp
from jax import lax
from jax.sharding import PartitionSpec as P

HEAD_DIM = 128
STATE = 256
BLOCK = 256
INNER = 16384


def shifted(shard, axis, by):
    length = lax.axis_size(axis)
    pairs = [(i, i + by) for i in range(length) if 0 <= i + by < length]
    return lax.ppermute(shard, axis, pairs)


def prefix(part, axis, combine, identity):
    place = lax.axis_index(axis)
    gathered = jax.tree.map(lambda a: lax.all_gather(a, axis), part)
    state = jax.tree.map(lambda a, e: jnp.zeros_like(a) + jnp.asarray(e, a.dtype), part, identity)

    def one(hop, state):
        return combine(
            state, jax.tree.map(lambda a: lax.dynamic_index_in_dim(a, hop, 0, False), gathered)
        )

    return lax.fori_loop(0, place, one, state)


def convolve_rows(padded, conv_weight, conv_bias):
    tap_count = conv_weight.shape[0]
    row_count = padded.shape[0] - tap_count + 1
    padded_float = padded.astype(jnp.float32)
    accumulated = jnp.broadcast_to(conv_bias[None, :], (row_count, padded.shape[1]))
    for offset in range(tap_count):
        accumulated = (
            accumulated + conv_weight[offset][None, :] * padded_float[offset : offset + row_count]
        )
    return jax.nn.silu(accumulated).astype(jnp.bfloat16)


def on_device(x_inner, z_gate, bc_raw, conv_weight, conv_bias, dt_raw, a_log, d_skip, norm_gain):
    highest = lax.Precision.HIGHEST
    rim_count = conv_weight.shape[0] - 1
    gathered = lax.all_gather(bc_raw, "head", axis=0, tiled=True)
    rim_rows = shifted(gathered[-rim_count:], "seq", 1)
    bc_act = convolve_rows(jnp.concatenate([rim_rows, gathered], axis=0), conv_weight, conv_bias)
    length = x_inner.shape[0]
    head_count = a_log.shape[0]
    block_count = length // BLOCK
    step_size = jax.nn.softplus(dt_raw)
    log_step = -jnp.exp(a_log)[None, :] * step_size
    cum_log = jnp.cumsum(log_step.reshape(block_count, BLOCK, head_count), axis=1)
    size_blocks = step_size.reshape(block_count, BLOCK, head_count)
    b_blocks = bc_act[:, :STATE].reshape(block_count, BLOCK, STATE)
    c_blocks = bc_act[:, STATE:].reshape(block_count, BLOCK, STATE)
    x_float = x_inner.astype(jnp.float32).reshape(block_count, BLOCK, head_count, HEAD_DIM)
    gram_blocks = jnp.einsum("cin,cjn->cij", c_blocks, b_blocks, preferred_element_type=jnp.float32)
    lower_mask = jnp.tril(jnp.ones((BLOCK, BLOCK), dtype=bool))
    by_head = jnp.transpose(cum_log, (0, 2, 1))
    spread = by_head[:, :, :, None] - by_head[:, :, None, :]
    decay_blocks = jnp.where(lower_mask, jnp.exp(jnp.where(lower_mask, spread, 0.0)), 0.0)
    weights = (
        gram_blocks[:, None] * decay_blocks * jnp.transpose(size_blocks, (0, 2, 1))[:, :, None, :]
    )
    inner_part = jnp.einsum("chij,cjhp->cihp", weights, x_float, precision=highest)
    tail_weight = jnp.exp(cum_log[:, -1:, :] - cum_log) * size_blocks
    block_states = jnp.einsum(
        "cjhp,cjn->chpn",
        x_float * tail_weight[..., None],
        b_blocks.astype(jnp.float32),
        precision=highest,
    )
    block_decay = jnp.exp(cum_log[:, -1, :])
    zero_state = jnp.zeros((head_count, HEAD_DIM, STATE), jnp.float32)
    starts = []
    current = zero_state
    for block_index in range(block_count):
        starts.append(current)
        current = block_decay[block_index][:, None, None] * current + block_states[block_index]
    zero_starts = jnp.stack(starts)
    log_total = jnp.sum(cum_log[:, -1, :], axis=0)

    def combine(earlier, later):
        return (earlier[0] + later[0], jnp.exp(later[0])[:, None, None] * earlier[1] + later[1])

    identity = (jnp.zeros_like(log_total), zero_state)
    chained = prefix((log_total, current), "seq", combine, identity)
    incoming = chained[1]
    c_float = c_blocks.astype(jnp.float32)
    carried_part = jnp.exp(cum_log)[..., None] * jnp.einsum(
        "cin,chpn->cihp", c_float, zero_starts, precision=highest
    )
    prior_log = jnp.cumsum(cum_log[:, -1, :], axis=0) - cum_log[:, -1, :]
    entry_part = jnp.exp(cum_log + prior_log[:, None, :])[..., None] * jnp.einsum(
        "cin,hpn->cihp", c_float, incoming, precision=highest
    )
    carried_part = carried_part + entry_part
    ssm_out = inner_part + carried_part + d_skip[None, None, :, None] * x_float
    gated_out = ssm_out.reshape(length, head_count * HEAD_DIM) * jax.nn.silu(
        z_gate.astype(jnp.float32)
    )
    square_sum = lax.psum(jnp.sum(gated_out * gated_out, axis=1), "head")
    inverse_rms = lax.rsqrt(square_sum / INNER + 1e-05)
    return (gated_out * inverse_rms[:, None] * norm_gain[None, :]).astype(jnp.bfloat16)


def solution(mesh):
    placed = (
        P("seq", "head"),
        P("seq", "head"),
        P(("seq", "head"), None),
        P(),
        P(),
        P("seq", "head"),
        P("head"),
        P("head"),
        P("head"),
    )
    return jax.shard_map(
        on_device, mesh=mesh, in_specs=placed, out_specs=P("seq", "head"), check_vma=False
    )
```

profile of v0, /device:TPU:22, one launch (start us, length us, event | category | flops | bytes accessed | tf_op | source)
XLA Modules:
  0.0 351.3 jit_solution(10148498477770559478)
XLA Ops:
  6.5 0.7 all-gather.4.cloned.1.call-update
  7.3 0.7 exponential_negate_fusion
  8.0 0.8 broadcast_multiply_fusion
  8.8 7.2 %reduce-window.6 = f32[6,4,2,128]{3,2,1,0:T(2,128)S(1)} reduce-window(f32[6,4,2,128]{3,2,1,0:T(2,128)S(1)} %copy.59, f32[]{:T(128)} %constant.42.clone.1), window={size=1x1x1x128 pad=0_0x0_0x0_0x127_0}, to_apply=%region_0.1 | reduce-window | flops 780288 | bytes 49156 | tf_op jit(solution)/shard_map/reduce-window
  16.7 0.2 subtract_reduce_fusion
  16.9 0.8 broadcast_dynamic-update-slice_fusion
  17.7 0.9 fusion.36
  18.7 127.5 %all-gather.4.cloned.1.call-done = bf16[1536,512]{1,0:T(8,128)(2,1)} async-done(((bf16[48,512]{1,0:T(8,128)(2,1)}), bf16[1536,512]{1,0:T(8,128)(2,1)}) %all-gather.4.cloned.1.call-update) | async-done | bytes 1572880 | tf_op jit(solution)/shard_map/all_gather | solution.py:46
  146.2 0.8 slice.108
  147.1 1.9 collective-permute-start
  149.0 0.3 slice_reduce_fusion.1
  149.2 2.4 reshape.86
  151.6 1.8 collective-permute-done
  153.5 0.5 maximum_convert_fusion
  154.0 2.0 multiply_convert_fusion.1
  156.1 4.3 %fusion.7 = f32[6,4,128,256]{3,2,1,0:T(8,128)S(1)} fusion(bf16[6,256,256,1]{2,1,3,0:T(8,128)(2,1)S(1)} %bitcast.69, f32[6,256,4]{1,2,0:T(4,128)S(1)} %copy.52, bf16[6,256,4,128]{3,2,1,0:T(4,128)(2,1)S(1)} %reshape.86), kind=kOutput, calls=%fused_computation.13 | convolution fusion | flops 2417491968 | bytes 5529600 | tf_op jit(solution)/shard_map/cjhp,cjn->chpn/dot_general | solution.py:69
  160.5 0.1 constant_dynamic-update-slice_fusion.1
  160.8 0.2 constant_dynamic-update-slice_fusion
  161.0 1.0 fusion.30
  162.0 1.8 copy-done.2
  163.8 1.3 dynamic-slice
  165.7 0.2 dynamic-update-slice
  165.9 27.4 %all-reduce = f32[64]{0:T(128)S(1)} all-reduce(f32[64]{0:T(128)S(1)} %dynamic-update-slice), channel_id=2, replica_groups=mesh['seq'=16,'head'=32] {'seq'}, use_global_device_ids=true, to_apply=%add | all-reduce | flops 64 | bytes 512
  193.5 0.4 fusion.37
  193.9 6.0 %fusion = f32[6,4,256,128]{3,2,1,0:T(8,128)} fusion(f32[6,4,256]{2,1,0:T(4,128)S(1)} %copy.47, f32[6,4,256]{2,1,0:T(4,128)S(1)} %reduce_window_sum.35, f32[6,256,256]{2,1,0:T(8,128)S(1)} %fusion.37, pred[256,256]{1,0:T(8,128)(4,1)S(1)} %iota_compare_fusion, bf16[6,256,4,128]{3,2,1,0:T(4,128)(2,1)S(1)} %reshape.86), kind=kOutput, calls=%fused_computation.2 | convolution fusion | flops 2423783424 | bytes 6406144 | tf_op jit(solution)/shard_map/chij,cjhp->cihp/dot_general | solution.py:67
  199.9 46.5 %all-gather.6.cloned.1.call-done = f32[16,4,128,256]{3,2,1,0:T(8,128)} async-done(((f32[1,4,128,256]{3,2,1,0:T(8,128)}), f32[16,4,128,256]{3,2,1,0:T(8,128)}) %all-gather.6.cloned.1.call-update) | async-done | bytes 8388624 | tf_op jit(solution)/shard_map/all_gather | solution.py:20
  246.4 17.7 %while.12 = (s32[]{:T(128)}, f32[4,128,256]{2,1,0:T(8,128)S(1)}, s32[]{:T(128)}, f32[16,4]{1,0:T(8,128)S(1)}, f32[16,4,128,256]{3,2,1,0:T(8,128)}, /*index=5*/s32[]{:T(128)}, s32[]{:T(128)}, s32[]{:T(128)}) while((s32[]{:T(128)}, f32[4,128,256]{2,1,0:T(8,128)S(1)}, s32[]{:T(128)}, f32[16,4]{1,0:T(8,128)S(1)}, f32[16,4,128,256]{3,2,1,0:T(8,128)}, ...), condition=%wide.region_5.6_spmd, body=%wide.region_4.5_spmd.sunk | while | flops 262149 | bytes 1573039 | solution.py:28
  246.5 1.2 bitcast_add_fusion.3
  247.7 1.2 bitcast_add_fusion.3
  249.0 1.2 bitcast_add_fusion.3
  250.2 1.2 bitcast_add_fusion.3
  251.5 1.2 bitcast_add_fusion.3
  252.7 1.2 bitcast_add_fusion.3
  254.0 1.2 bitcast_add_fusion.3
  255.2 1.2 bitcast_add_fusion.3
  256.5 1.2 bitcast_add_fusion.3
  257.7 1.2 bitcast_add_fusion.3
  259.0 1.2 bitcast_add_fusion.3
  260.2 1.2 bitcast_add_fusion.3
  261.5 1.2 bitcast_add_fusion.3
  262.7 1.2 bitcast_add_fusion.3
  264.1 1.5 fusion.26
  265.6 0.4 copy-done.3
  266.0 5.3 %fusion.8 = f32[6,256,4,128]{3,1,2,0:T(8,128)S(1)} fusion(f32[6,4,256,128]{3,2,1,0:T(8,128)} %fusion, f32[6,256,4,128]{3,1,2,0:T(8,128)S(1)} %fusion.26, bf16[6,256,256,1]{2,1,3,0:T(8,128)(2,1)S(1)} %bitcast.68, f32[6,4,128,256]{3,2,1,0:T(8,128)S(1)} %copy-done.3, f32[4]{0:T(128)S(1)} %copy-done.7, f32[6,256,4]{1,2,0:T(4,128)S(1)} %copy.54, ...), kind=kOutput, calls=%fused_computation.14 | convolution fusion | flops 2421424128 | bytes 14991376 | tf_op jit(solution)/shard_map/cin,chpn->cihp/dot_general | solution.py:92
  271.3 2.0 copy.55
  273.4 1.0 multiply_reduce_fusion
  274.4 66.5 %psum.7 = f32[1536]{0:T(1024)S(1)} all-reduce(f32[1536]{0:T(1024)S(1)} %multiply_reduce_fusion), channel_id=1, replica_groups=mesh['seq'=16,'head'=32] {'head'}, use_global_device_ids=true, to_apply=%region_7.8 | all-reduce | flops 1536 | bytes 12288 | tf_op jit(solution)/shard_map/psum | solution.py:104
  341.0 3.5 multiply_convert_fusion
  (59 shorter events, 1.6 us)
Async XLA Ops:
  6.5 139.7 %all-gather.4.cloned.1.call-start = ((), (), s32[]{:S(2)}) async-start(), calls=%async_computation | async-start | bytes 1622016 | tf_op jit(solution)/shard_map/all_gather | solution.py:46
  7.3 239.1 %all-gather.6.cloned.1.call-start = ((), (), s32[]{:S(2)}) async-start(), calls=%async_computation.1 | async-start | bytes 8912896 | tf_op jit(solution)/shard_map/all_gather | solution.py:20
  146.2 7.2 %copy-start.4 = (bf16[1536,512]{1,0:T(8,128)(2,1)S(1)}, bf16[1536,512]{1,0:T(8,128)(2,1)}, u32[]{:S(2)}) copy-start(bf16[1536,512]{1,0:T(8,128)(2,1)} %all-gather.4.cloned.1.call-done) | copy-start | bytes 4718596
  147.1 6.4 %collective-permute-start = (bf16[3,512]{1,0:T(4,128)(2,1)S(1)}, bf16[3,512]{1,0:T(4,128)(2,1)S(1)}, u32[]{:S(2)}, u32[]{:S(2)}) collective-permute-start(bf16[3,512]{1,0:T(4,128)(2,1)S(1)} %slice.108), channel_id=1, source_target_pairs={{0,32},{32,64},{64,96},{96,128},{128,160},{160,192},{192,224},{224... | collective-permute-start | bytes 9224 | tf_op jit(solution)/shard_map/ppermute | solution.py:15
  151.6 2.3 copy-start.5
  156.1 4.3 %copy-start.1 = (f32[6,4,128,256]{3,2,1,0:T(8,128)S(1)}, f32[6,4,128,256]{3,2,1,0:T(8,128)}, u32[]{:S(2)}) copy-start(f32[6,4,128,256]{3,2,1,0:T(8,128)} %broadcast_dynamic-update-slice_fusion) | copy-start | bytes 9437188
  162.0 1.8 copy-start.2
  264.1 1.9 copy-start.3
  264.1 1.9 copy-start.7
  271.3 2.1 copy-start
  273.3 67.6 %copy-start.6 = (f32[512]{0:T(512)S(1)}, f32[512]{0:T(512)}, u32[]{:S(2)}) copy-start(f32[512]{0:T(512)} %param.19) | copy-start | bytes 6148
Sparse Core Ops, SparseCore 0:
  9.4 136.7 all-gather.3
  163.9 82.4 all-gather.5
where the time goes:
time: 352 us; the launch traced here: 351 us
  waiting for transfers between devices  177 us (50%)
  blocking collectives  93.9 us (27%)
  other arithmetic  34.8 us (10%)
  matrix products  17.5 us (5%)
  between operations  14.4 us (4%)
  local copies, waits for them, and re-layouts  11.6 us (3%)
    all_gather x1, waiting for transfers between devices, on_device(): gathered = lax.all_gather(bc_raw, 'head', axis=0, tiled=True)  128 us
    psum x1, blocking collectives, on_device(): square_sum = lax.psum(jnp.sum(gated_out * gated_out, axis=1), 'head')  66.5 us
    all_gather x1, waiting for transfers between devices, prefix(): gathered = jax.tree.map(lambda a: lax.all_gather(a, axis), part)  46.5 us
    unnamed x1, blocking collectives  27.4 us
    add x14, other arithmetic, combine(): jnp.exp(later[0])[:, None, None] * earlier[1] + later[1]  16.8 us
    another operation x3, other arithmetic  7.34 us
  transfers between devices with their start and end apart: 3, of which 3 were waited for; matrix products, arithmetic and copies ran while one was open for 6% of the time, Pallas kernels for 0%

commit v1 on v0

--- a/solution.py
+++ b/solution.py
@@ -101,7 +101,7 @@
     gated_out = ssm_out.reshape(length, head_count * HEAD_DIM) * jax.nn.silu(
         z_gate.astype(jnp.float32)
     )
-    square_sum = lax.psum(jnp.sum(gated_out * gated_out, axis=1), "head")
+    square_sum = jnp.sum(lax.all_gather(jnp.sum(gated_out * gated_out, axis=1), "head"), axis=0)
     inverse_rms = lax.rsqrt(square_sum / INNER + 1e-05)
     return (gated_out * inverse_rms[:, None] * norm_gain[None, :]).astype(jnp.bfloat16)
 

time: 352 us -> 352 us (level)
    psum x1 -> x0, blocking collectives: 66.5 us -> none  [on_device(): square_sum = lax.psum(jnp.sum(gated_out * gated_out, axis=1), 'head')]
    all_gather x0 -> x1, blocking collectives: none -> 65 us  [on_device(): lax.all_gather(jnp.sum(gated_out * gated_out, axis=1), 'head')]
  transfers between devices with their start and end apart: 3 -> 3, of which waited for: 3 -> 3; matrix products, arithmetic and copies ran while one was open for 6% -> 7% of each run, Pallas kernels for 0% -> 0%
where the time goes in v1:
time: 352 us; the launch traced here: 351 us
  waiting for transfers between devices  175 us (50%)
  blocking collectives  92.4 us (26%)
  other arithmetic  36.3 us (10%)
  matrix products  18.7 us (5%)
  between operations  14.4 us (4%)
  local copies, waits for them, and re-layouts  11.5 us (3%)
    all_gather x1, waiting for transfers between devices, on_device(): gathered = lax.all_gather(bc_raw, 'head', axis=0, tiled=True)  128 us
    all_gather x1, blocking collectives, on_device(): lax.all_gather(jnp.sum(gated_out * gated_out, axis=1), 'head')  65 us
    all_gather x1, waiting for transfers between devices, prefix(): gathered = jax.tree.map(lambda a: lax.all_gather(a, axis), part)  45.3 us
    unnamed x1, blocking collectives  27.4 us
    add x14, other arithmetic, combine(): jnp.exp(later[0])[:, None, None] * earlier[1] + later[1]  16.8 us
    another operation x3, other arithmetic  7.34 us
  transfers between devices with their start and end apart: 3, of which 3 were waited for; matrix products, arithmetic and copies ran while one was open for 7% of the time, Pallas kernels for 0%

profile of v1, /device:TPU:22, one launch (start us, length us, event | category | flops | bytes accessed | tf_op | source)
XLA Modules:
  0.0 351.3 jit_solution(9306907876210233286)
XLA Ops:
  6.5 0.7 all-gather.6.cloned.1.call-update
  7.3 0.7 exponential_negate_fusion
  8.0 0.8 broadcast_multiply_fusion
  8.8 7.2 %reduce-window.6 = f32[6,4,2,128]{3,2,1,0:T(2,128)S(1)} reduce-window(f32[6,4,2,128]{3,2,1,0:T(2,128)S(1)} %copy.59, f32[]{:T(128)} %constant.42.clone.1), window={size=1x1x1x128 pad=0_0x0_0x0_0x127_0}, to_apply=%region_0.1 | reduce-window | flops 780288 | bytes 49156 | tf_op jit(solution)/shard_map/reduce-window
  16.7 0.2 subtract_reduce_fusion
  16.9 0.8 broadcast_dynamic-update-slice_fusion
  17.7 0.9 fusion.36
  18.7 127.5 %all-gather.6.cloned.1.call-done = bf16[1536,512]{1,0:T(8,128)(2,1)} async-done(((bf16[48,512]{1,0:T(8,128)(2,1)}), bf16[1536,512]{1,0:T(8,128)(2,1)}) %all-gather.6.cloned.1.call-update) | async-done | bytes 1572880 | tf_op jit(solution)/shard_map/all_gather | solution.py:46
  146.2 0.7 slice.108
  146.9 1.9 collective-permute-start
  148.8 0.3 slice_reduce_fusion.1
  149.1 2.4 reshape.90
  151.5 1.8 collective-permute-done
  153.4 1.9 maximum_convert_fusion
  155.2 2.0 multiply_convert_fusion.1
  157.4 4.4 %fusion.7 = f32[6,4,128,256]{3,2,1,0:T(8,128)S(1)} fusion(bf16[6,256,256,1]{2,1,3,0:T(8,128)(2,1)S(1)} %bitcast.69, f32[6,256,4]{1,2,0:T(4,128)S(1)} %copy.52, bf16[6,256,4,128]{3,2,1,0:T(4,128)(2,1)S(1)} %reshape.90), kind=kOutput, calls=%fused_computation.13 | convolution fusion | flops 2417491968 | bytes 5529600 | tf_op jit(solution)/shard_map/cjhp,cjn->chpn/dot_general | solution.py:69
  161.9 0.1 constant_dynamic-update-slice_fusion.1
  162.2 0.2 constant_dynamic-update-slice_fusion
  162.4 1.0 fusion.30
  163.4 1.8 copy-done.3
  165.2 1.3 dynamic-slice
  167.1 0.2 dynamic-update-slice
  167.3 27.4 %all-reduce = f32[64]{0:T(128)S(1)} all-reduce(f32[64]{0:T(128)S(1)} %dynamic-update-slice), channel_id=2, replica_groups=mesh['seq'=16,'head'=32] {'seq'}, use_global_device_ids=true, to_apply=%add | all-reduce | flops 64 | bytes 512
  194.9 1.5 fusion.37
  196.4 6.0 %fusion = f32[6,4,256,128]{3,2,1,0:T(8,128)} fusion(f32[6,4,256]{2,1,0:T(4,128)S(1)} %copy.47, f32[6,4,256]{2,1,0:T(4,128)S(1)} %reduce_window_sum.35, f32[6,256,256]{2,1,0:T(8,128)S(1)} %fusion.37, pred[256,256]{1,0:T(8,128)(4,1)S(1)} %iota_compare_fusion, bf16[6,256,4,128]{3,2,1,0:T(4,128)(2,1)S(1)} %reshape.90), kind=kOutput, calls=%fused_computation.2 | convolution fusion | flops 2423783424 | bytes 6406144 | tf_op jit(solution)/shard_map/chij,cjhp->cihp/dot_general | solution.py:67
  202.4 45.3 %all-gather.8.cloned.1.call-done = f32[16,4,128,256]{3,2,1,0:T(8,128)} async-done(((f32[1,4,128,256]{3,2,1,0:T(8,128)}), f32[16,4,128,256]{3,2,1,0:T(8,128)}) %all-gather.8.cloned.1.call-update) | async-done | bytes 8388624 | tf_op jit(solution)/shard_map/all_gather | solution.py:20
  247.8 17.7 %while.12 = (s32[]{:T(128)}, f32[4,128,256]{2,1,0:T(8,128)S(1)}, s32[]{:T(128)}, f32[16,4]{1,0:T(8,128)S(1)}, f32[16,4,128,256]{3,2,1,0:T(8,128)}, /*index=5*/s32[]{:T(128)}, s32[]{:T(128)}, s32[]{:T(128)}) while((s32[]{:T(128)}, f32[4,128,256]{2,1,0:T(8,128)S(1)}, s32[]{:T(128)}, f32[16,4]{1,0:T(8,128)S(1)}, f32[16,4,128,256]{3,2,1,0:T(8,128)}, ...), condition=%wide.region_5.6_spmd, body=%wide.region_4.5_spmd.sunk | while | flops 262149 | bytes 1573039 | solution.py:28
  247.9 1.2 bitcast_add_fusion.3
  249.1 1.2 bitcast_add_fusion.3
  250.4 1.2 bitcast_add_fusion.3
  251.6 1.2 bitcast_add_fusion.3
  252.9 1.2 bitcast_add_fusion.3
  254.1 1.2 bitcast_add_fusion.3
  255.4 1.2 bitcast_add_fusion.3
  256.6 1.2 bitcast_add_fusion.3
  257.9 1.2 bitcast_add_fusion.3
  259.1 1.2 bitcast_add_fusion.3
  260.4 1.2 bitcast_add_fusion.3
  261.6 1.2 bitcast_add_fusion.3
  262.9 1.2 bitcast_add_fusion.3
  264.1 1.2 bitcast_add_fusion.3
  265.5 1.5 fusion.26
  267.0 0.4 copy-done.4
  267.4 5.3 %fusion.8 = f32[6,256,4,128]{3,1,2,0:T(8,128)S(1)} fusion(f32[6,4,256,128]{3,2,1,0:T(8,128)} %fusion, f32[6,256,4,128]{3,1,2,0:T(8,128)S(1)} %fusion.26, bf16[6,256,256,1]{2,1,3,0:T(8,128)(2,1)S(1)} %bitcast.68, f32[6,4,128,256]{3,2,1,0:T(8,128)S(1)} %copy-done.4, f32[4]{0:T(128)S(1)} %copy-done.7, f32[6,256,4]{1,2,0:T(4,128)S(1)} %copy.54, ...), kind=kOutput, calls=%fused_computation.14 | convolution fusion | flops 2421424128 | bytes 14991376 | tf_op jit(solution)/shard_map/cin,chpn->cihp/dot_general | solution.py:92
  272.7 2.0 copy.55
  274.8 1.0 multiply_reduce_fusion
  275.8 65.0 %all-gather.2 = f32[32,1,1536]{2,1,0:T(1,128)S(1)} all-gather(f32[1,1,1536]{2,1,0:T(1,128)S(1)} %reshape.98), channel_id=3, replica_groups=mesh['seq'=16,'head'=32] {'head'}, dimensions={0}, use_global_device_ids=true | all-gather | bytes 202752 | tf_op jit(solution)/shard_map/all_gather | solution.py:104
  340.9 3.5 multiply_convert_fusion
  (61 shorter events, 1.7 us)
Async XLA Ops:
  6.5 139.7 %all-gather.6.cloned.1.call-start = ((), (), s32[]{:S(2)}) async-start(), calls=%async_computation | async-start | bytes 1622016 | tf_op jit(solution)/shard_map/all_gather | solution.py:46
  7.3 240.5 %all-gather.8.cloned.1.call-start = ((), (), s32[]{:S(2)}) async-start(), calls=%async_computation.1 | async-start | bytes 8912896 | tf_op jit(solution)/shard_map/all_gather | solution.py:20
  146.9 6.4 %collective-permute-start = (bf16[3,512]{1,0:T(4,128)(2,1)S(1)}, bf16[3,512]{1,0:T(4,128)(2,1)S(1)}, u32[]{:S(2)}, u32[]{:S(2)}) collective-permute-start(bf16[3,512]{1,0:T(4,128)(2,1)S(1)} %slice.108), channel_id=1, source_target_pairs={{0,32},{32,64},{64,96},{96,128},{128,160},{160,192},{192,224},{224... | collective-permute-start | bytes 9224 | tf_op jit(solution)/shard_map/ppermute | solution.py:15
  151.5 3.7 %copy-start.5 = (f32[512]{0:T(512)S(1)}, f32[512]{0:T(512)}, u32[]{:S(2)}) copy-start(f32[512]{0:T(512)} %param.15) | copy-start | bytes 6148
  157.4 6.0 %copy-start = (bf16[1536,256]{1,0:T(8,128)(2,1)}, bf16[1536,256]{1,0:T(8,128)(2,1)S(1)}, u32[]{:S(2)}) copy-start(bf16[1536,256]{1,0:T(8,128)(2,1)S(1)} %get-tuple-element.75) | copy-start | bytes 2359300
  157.4 4.4 %copy-start.2 = (f32[6,4,128,256]{3,2,1,0:T(8,128)S(1)}, f32[6,4,128,256]{3,2,1,0:T(8,128)}, u32[]{:S(2)}) copy-start(f32[6,4,128,256]{3,2,1,0:T(8,128)} %broadcast_dynamic-update-slice_fusion) | copy-start | bytes 9437188
  163.4 1.8 copy-start.3
  265.5 1.9 copy-start.4
  265.5 1.9 copy-start.7
  272.7 2.1 copy-start.1
  274.7 66.2 %copy-start.6 = (f32[512]{0:T(512)S(1)}, f32[512]{0:T(512)}, u32[]{:S(2)}) copy-start(f32[512]{0:T(512)} %param.19) | copy-start | bytes 6148
Sparse Core Ops, SparseCore 0:
  9.4 136.7 all-gather.5
  165.3 82.4 all-gather.7
